TPU v7x, 32 devices: a whole 2x2x4 slice. The times are simulated.
32 devices in a mesh: groups: 2 (over x), seq: 16 (over z, y, core).
Axes of the slice: x: 2, y: 2, z: 4, core: 2. Of those that a mesh axis runs over, the one named last changes fastest.
Arguments:
- tokens: bfloat16 [32768, 1024], P(('groups', 'seq')), parts along dimension 0, may hold values from -6 to 6
- cotangent: bfloat16 [32768, 1024], P(('groups', 'seq')), parts along dimension 0, may hold values from -6 to 6
- gate_weight: bfloat16 [1024, 1024], P('seq'), may hold values from -0.1875 to 0.1875
- left_blocks: bfloat16 [32, 512, 512], P('seq'), may hold values from -0.25 to 0.25
- right_blocks: bfloat16 [512, 32, 32], P('seq'), may hold values from -1 to 1
Outputs:
- output: bfloat16 [32768, 1024], P(('groups', 'seq')), parts along dimension 0
- input_grad: bfloat16 [32768, 1024], P(('groups', 'seq')), parts along dimension 0
- gate_grad: float32 [2048, 1024], P(('groups', 'seq')), parts along dimension 0
- left_grad: bfloat16 [64, 512, 512], P(('groups', 'seq')), parts along dimension 0
- right_grad: bfloat16 [1024, 32, 32], P(('groups', 'seq')), parts along dimension 0
There are 2 independent parts, one for each index of `groups`. A program takes and returns all parts, laid end to end along the dimension named above; an argument that names none is the same for every part. Nothing has to cross between parts.
All inputs are finite; a program needn't handle non-finite values.
Results may differ from a plain program's by a relative error of at most 0.0095.
Values may be sent and summed in bfloat16 or wider, within the bound.
A program may use at most 128 MiB of HBM per device.

v0:
```python
import jax
import jax.numpy as jnp
from jax import lax
from jax.sharding import PartitionSpec as P


def silu_slope(value):
    sig = jax.nn.sigmoid(value)
    return sig * (1.0 + value * (1.0 - sig))


def to_columns(values):
    return lax.all_to_all(values, "seq", split_axis=1, concat_axis=0, tiled=True)


def to_rows(values):
    return lax.all_to_all(values, "seq", split_axis=0, concat_axis=1, tiled=True)


def body(tokens, cotangent, gate_weight, left_blocks, right_blocks):
    seq_count = lax.axis_size("seq")
    local_blocks = left_blocks.shape[0]
    block_size = left_blocks.shape[1]
    tok_rows = tokens.shape[0]
    channels = tokens.shape[1]
    token_grid = tokens.reshape(local_blocks, block_size, channels)
    upstream = cotangent.reshape(local_blocks, block_size, channels)
    first = jnp.einsum(
        "ajb,abc->ajc", left_blocks, token_grid, preferred_element_type=jnp.float32
    ).astype(jnp.bfloat16)
    full_weight = lax.all_gather(gate_weight, "seq", axis=0, tiled=True)
    gate_sum = jnp.dot(tokens, full_weight, preferred_element_type=jnp.float32)
    gate = gate_sum.astype(jnp.bfloat16).reshape(local_blocks, block_size, channels)
    first_cols = to_columns(first)
    second_cols = jnp.einsum(
        "bia,abc->ibc", right_blocks, first_cols, preferred_element_type=jnp.float32
    ).astype(jnp.bfloat16)
    second = to_rows(second_cols)
    gate_f = gate.astype(jnp.float32)
    factor = jax.nn.silu(gate_f)
    second_f = second.astype(jnp.float32)
    upstream_f = upstream.astype(jnp.float32)
    output = (second_f * factor).astype(jnp.bfloat16)
    second_grad = (upstream_f * factor).astype(jnp.bfloat16)
    gate_delta = (upstream_f * second_f * silu_slope(gate_f)).astype(jnp.bfloat16)
    grad_cols = to_columns(second_grad)
    first_grad_cols = jnp.einsum(
        "bia,ibc->abc", right_blocks, grad_cols, preferred_element_type=jnp.float32
    ).astype(jnp.bfloat16)
    scale_w = channels ** (-0.5)
    right_grad = (
        jnp.einsum("ibc,abc->bia", grad_cols, first_cols, preferred_element_type=jnp.float32)
        * scale_w
    ).astype(jnp.bfloat16)
    first_grad = to_rows(first_grad_cols)
    left_grad = (
        jnp.einsum("ajc,abc->ajb", first_grad, token_grid, preferred_element_type=jnp.float32)
        * scale_w
    ).astype(jnp.bfloat16)
    mixer_part = jnp.einsum(
        "ajb,ajc->abc", left_blocks, first_grad, preferred_element_type=jnp.float32
    ).reshape(tok_rows, channels)
    delta_flat = gate_delta.reshape(tok_rows, channels)
    gate_part = jnp.einsum("tc,kc->tk", delta_flat, full_weight, preferred_element_type=jnp.float32)
    input_grad = (mixer_part + gate_part).astype(jnp.bfloat16)
    weight_term = jnp.einsum("tk,tc->kc", tokens, delta_flat, preferred_element_type=jnp.float32)
    gate_grad = lax.psum_scatter(weight_term, "seq", scatter_dimension=0, tiled=True)
    gate_grad = gate_grad * (tok_rows * seq_count) ** (-0.5)
    return (output.reshape(tok_rows, channels), input_grad, gate_grad, left_grad, right_grad)


def solution(mesh):
    in_specs = (
        P(("groups", "seq"), None),
        P(("groups", "seq"), None),
        P("seq", None),
        P("seq", None, None),
        P("seq", None, None),
    )
    out_specs = (
        P(("groups", "seq"), None),
        P(("groups", "seq"), None),
        P(("groups", "seq"), None),
        P(("groups", "seq"), None, None),
        P(("groups", "seq"), None, None),
    )
    return jax.shard_map(body, mesh=mesh, in_specs=in_specs, out_specs=out_specs, check_vma=False)
```

profile of v0, /device:TPU:13, one launch (start us, length us, event | category | flops | bytes accessed | tf_op | source)
XLA Modules:
  0.0 312.8 jit_solution(347936840301729798)
XLA Ops:
  7.2 1.6 copy-done
  8.8 2.5 convolution_convert_fusion.1
  11.2 2.2 copy.30
  13.4 53.7 %all_to_all.63 = bf16[2,512,1024]{2,0,1:T(2,128)(2,1)S(1)} all-to-all(bf16[2,512,1024]{2,0,1:T(2,128)(2,1)S(1)} %copy.30), channel_id=1, replica_groups=mesh['groups'=2,'seq'=16] {'seq'}, dimensions={1} | all-to-all | bytes 4194304 | tf_op jit(solution)/shard_map/all_to_all | solution.py:13
  67.1 3.5 %copy.48 = bf16[2,16,32,1024]{3,0,1,2:T(2,128)(2,1)} copy(bf16[2,16,32,1024]{3,0,2,1:T(2,128)(2,1)S(1)} %bitcast.69) | data formatting | bytes 4194304 | tf_op jit(solution)/shard_map/all_to_all | solution.py:13
  70.6 4.2 %all_to_all.49 = bf16[32,32,1024]{2,0,1:T(8,128)(2,1)} reshape(bf16[16,2,32,1024]{3,1,0,2:T(2,128)(2,1)} %bitcast.70) | data formatting | bytes 4194304 | tf_op jit(solution)/shard_map/all_to_all | solution.py:13
  74.8 2.3 convert_bitcast_fusion.1
  77.1 2.5 copy.32
  79.5 5.1 %all-to-all-start.1 = ((bf16[32,32,1024]{2,1,0:T(8,128)(2,1)}), bf16[32,32,1024]{2,1,0:T(8,128)(2,1)}, u32[]{:S(2)}, u32[]{:S(2)}) async-start(bf16[32,32,1024]{2,1,0:T(8,128)(2,1)} %copy.32), calls=%async_computation.1 | async-start | bytes 4194304 | tf_op jit(solution)/shard_map/all_to_all | solution.py:17
  85.4 59.4 %all-to-all-done.1 = bf16[32,32,1024]{2,1,0:T(8,128)(2,1)} async-done(((bf16[32,32,1024]{2,1,0:T(8,128)(2,1)}), bf16[32,32,1024]{2,1,0:T(8,128)(2,1)}, u32[]{:S(2)}, u32[]{:S(2)}) %all-to-all-start.1) | async-done | bytes 2097184 | tf_op jit(solution)/shard_map/all_to_all | solution.py:17
  144.8 4.0 %copy.33 = f32[16,2,32,1024]{3,2,0,1:T(8,128)} copy(bf16[16,2,32,1024]{3,2,1,0:T(8,128)(2,1)} %bitcast.21) | data formatting | bytes 6291456 | tf_op jit(solution)/shard_map/convert_element_type | solution.py:41
  148.9 8.1 %fusion.3 = (bf16[1024,1024]{1,0:T(8,128)(2,1)}, bf16[1024,1024]{1,0:T(8,128)(2,1)}, bf16[1024,1024]{1,0:T(8,128)(2,1)S(1)}) fusion(f32[16,2,32,1024]{3,2,0,1:T(8,128)} %copy.33, bf16[1024,1024]{1,0:T(8,128)(2,1)} %param.6, bf16[1024,1024]{1,0:T(8,128)(2,1)S(1)} %copy-done, bf16[1024,1024]{1,0:T(8,128)(2,1)} %all-gather.2.cloned.1.call-done), kind=kOutput, calls=%fused_computation.6 | convolution fusion | flops 2164260864 | bytes 16777216 | tf_op jit(solution)/shard_map/dot_general | solution.py:32
  157.0 1.3 multiply_convert_fusion
  158.4 3.5 %copy.34 = bf16[2,512,1024]{2,0,1:T(2,128)(2,1)} copy(bf16[2,512,1024]{2,1,0:T(8,128)(2,1)S(1)} %multiply_convert_fusion) | data formatting | bytes 4194304 | tf_op jit(solution)/shard_map/convert_element_type | solution.py:44
  161.8 4.9 %all-to-all-start.2 = ((bf16[2,512,1024]{2,0,1:T(2,128)(2,1)}), bf16[2,512,1024]{2,0,1:T(2,128)(2,1)}, u32[]{:S(2)}, u32[]{:S(2)}) async-start(bf16[2,512,1024]{2,0,1:T(2,128)(2,1)} %copy.34), calls=%async_computation.2 | async-start | bytes 4194304 | tf_op jit(solution)/shard_map/all_to_all | solution.py:13
  167.0 6.0 %convolution_bitcast_fusion = f32[1024,1024]{0,1:T(8,128)} fusion(bf16[1024,1024]{1,0:T(8,128)(2,1)} %get-tuple-element.20, bf16[1024,1024]{1,0:T(8,128)(2,1)S(1)} %copy-done), kind=kOutput, calls=%fused_computation.9 | convolution fusion | flops 2147483648 | bytes 8388608 | tf_op jit(solution)/shard_map/tk,tc->kc/dot_general | solution.py:66
  172.9 5.4 %copy.43 = f32[1024,1024]{1,0:T(8,128)} copy(f32[1024,1024]{0,1:T(8,128)} %convolution_bitcast_fusion) | data formatting | bytes 8388608
  178.3 44.3 %all-to-all-done.2 = bf16[2,512,1024]{2,0,1:T(2,128)(2,1)} async-done(((bf16[2,512,1024]{2,0,1:T(2,128)(2,1)}), bf16[2,512,1024]{2,0,1:T(2,128)(2,1)}, u32[]{:S(2)}, u32[]{:S(2)}) %all-to-all-start.2) | async-done | bytes 2097184 | tf_op jit(solution)/shard_map/all_to_all | solution.py:13
  222.6 5.1 %copy.47 = bf16[2,16,32,1024]{3,0,1,2:T(2,128)(2,1)} copy(bf16[2,16,32,1024]{3,0,2,1:T(2,128)(2,1)} %bitcast.9) | data formatting | bytes 4194304 | tf_op jit(solution)/shard_map/all_to_all | solution.py:13
  227.7 4.2 %all_to_all.54 = bf16[32,32,1024]{2,0,1:T(8,128)(2,1)} reshape(bf16[16,2,32,1024]{3,1,0,2:T(2,128)(2,1)} %bitcast.71) | data formatting | bytes 4194304 | tf_op jit(solution)/shard_map/all_to_all | solution.py:13
  231.9 2.4 convert_bitcast_fusion
  234.3 2.5 copy.37
  236.8 5.4 %all-to-all-start.3 = ((bf16[32,32,1024]{2,1,0:T(8,128)(2,1)}), bf16[32,32,1024]{2,1,0:T(8,128)(2,1)}, u32[]{:S(2)}, u32[]{:S(2)}) async-start(bf16[32,32,1024]{2,1,0:T(8,128)(2,1)} %copy.37), calls=%async_computation.3 | async-start | bytes 4194304 | tf_op jit(solution)/shard_map/all_to_all | solution.py:17
  242.2 3.6 %fusion.4 = bf16[32,32,32]{2,1,0:T(8,128)(2,1)} fusion(bf16[32,32,1024]{2,0,1:T(8,128)(2,1)} %all_to_all.54, bf16[32,32,1024]{2,0,1:T(8,128)(2,1)} %all_to_all.49), kind=kOutput, calls=%fused_computation.18 | convolution fusion | flops 67174400 | bytes 4259840 | tf_op jit(solution)/shard_map/ibc,abc->bia/dot_general | solution.py:52
  245.8 18.3 %reduce-scatter.4.cloned.1.call-done = f32[64,1024]{1,0:T(8,128)} async-done(((f32[1024,1024]{1,0:T(8,128)}), f32[64,1024]{1,0:T(8,128)}) %reduce-scatter.4.cloned.1.call-update) | async-done | bytes 262160
  264.1 1.1 copy.44
  265.3 0.9 copy.40
  266.2 29.6 %all-to-all-done.3 = bf16[32,32,1024]{2,1,0:T(8,128)(2,1)} async-done(((bf16[32,32,1024]{2,1,0:T(8,128)(2,1)}), bf16[32,32,1024]{2,1,0:T(8,128)(2,1)}, u32[]{:S(2)}, u32[]{:S(2)}) %all-to-all-start.3) | async-done | bytes 2097184 | tf_op jit(solution)/shard_map/all_to_all | solution.py:17
  295.8 1.8 copy.38
  297.7 2.4 multiply_convert_fusion.1
  300.0 1.3 fusion.5
  302.2 3.7 %fusion = bf16[1024,1024]{1,0:T(8,128)(2,1)} fusion(f32[2,1024,512]{1,2,0:T(8,128)S(1)} %fusion.5, bf16[1024,1024]{1,0:T(8,128)(2,1)S(1)} %copy-done.5, bf16[1024,1024]{1,0:T(8,128)(2,1)S(1)} %copy-done.4), kind=kOutput, calls=%fused_computation.1 | convolution fusion | flops 2149580800 | bytes 10485760 | tf_op jit(solution)/shard_map/tc,kc->tk/dot_general | solution.py:64
  (17 shorter events, 2.0 us)
Async XLA Ops:
  7.2 1.6 copy-start
  70.6 4.2 %copy-start.3 = (bf16[32,32,32]{2,1,0:T(8,128)(2,1)S(1)}, bf16[32,32,32]{2,1,0:T(8,128)(2,1)}, u32[]{:S(2)}) copy-start(bf16[32,32,32]{2,1,0:T(8,128)(2,1)} %param.9) | copy-start | bytes 196612
  79.5 65.3 %all-to-all-start.1 = ((bf16[32,32,1024]{2,1,0:T(8,128)(2,1)}), bf16[32,32,1024]{2,1,0:T(8,128)(2,1)}, u32[]{:S(2)}, u32[]{:S(2)}) async-start(bf16[32,32,1024]{2,1,0:T(8,128)(2,1)} %copy.32), calls=%async_computation.1 | async-start | bytes 4194304 | tf_op jit(solution)/shard_map/all_to_all | solution.py:17
  84.7 64.2 %all-gather.2.cloned.1.call-start = ((), (), s32[]{:S(2)}) async-start(), calls=%async_computation.5 | async-start | bytes 2228224 | tf_op jit(solution)/shard_map/all_gather | solution.py:31
  148.9 8.1 %copy-start.1 = (bf16[1024,1024]{1,0:T(8,128)(2,1)S(1)}, bf16[1024,1024]{1,0:T(8,128)(2,1)}, u32[]{:S(2)}) copy-start(bf16[1024,1024]{1,0:T(8,128)(2,1)} %param.6) | copy-start | bytes 6291460
  161.8 60.8 %all-to-all-start.2 = ((bf16[2,512,1024]{2,0,1:T(2,128)(2,1)}), bf16[2,512,1024]{2,0,1:T(2,128)(2,1)}, u32[]{:S(2)}, u32[]{:S(2)}) async-start(bf16[2,512,1024]{2,0,1:T(2,128)(2,1)} %copy.34), calls=%async_computation.2 | async-start | bytes 4194304 | tf_op jit(solution)/shard_map/all_to_all | solution.py:13
  166.7 97.4 %reduce-scatter.4.cloned.1.call-start = ((), (), s32[]{:S(2)}) async-start(), calls=%async_computation.6 | async-start | bytes 4456448
  236.8 59.0 %all-to-all-start.3 = ((bf16[32,32,1024]{2,1,0:T(8,128)(2,1)}), bf16[32,32,1024]{2,1,0:T(8,128)(2,1)}, u32[]{:S(2)}, u32[]{:S(2)}) async-start(bf16[32,32,1024]{2,1,0:T(8,128)(2,1)} %copy.37), calls=%async_computation.3 | async-start | bytes 4194304 | tf_op jit(solution)/shard_map/all_to_all | solution.py:17
  297.6 2.4 copy-start.2
  300.0 1.6 copy-start.4
  300.0 2.2 copy-start.5
Sparse Core Ops, SparseCore 0:
  87.6 57.0 all-gather.1
  178.4 85.6 reduce-scatter.3
where the time goes:
time: 314 us; the launch traced here: 313 us
  waiting for transfers between devices  152 us (48%)
  blocking collectives  53.7 us (17%)
  local copies, waits for them, and re-layouts  43.4 us (14%)
  matrix products  32.2 us (10%)
  starting transfers between devices  15.9 us (5%)
  between operations  14.1 us (4%)
    all_to_all x2, waiting for transfers between devices, to_rows(): lax.all_to_all(values, 'seq', split_axis=0, concat_axis=1, tiled=True)  89 us
    all_to_all x1, blocking collectives, to_columns(): lax.all_to_all(values, 'seq', split_axis=1, concat_axis=0, tiled=True)  53.7 us
    all_to_all x1, waiting for transfers between devices, to_columns(): lax.all_to_all(values, 'seq', split_axis=1, concat_axis=0, tiled=True)  44.3 us
    unnamed x3, waiting for transfers between devices  18.9 us
    all_to_all x4, local copies, waits for them, and re-layouts, to_columns(): lax.all_to_all(values, 'seq', split_axis=1, concat_axis=0, tiled=True)  17 us
    all_to_all x2, starting transfers between devices, to_rows(): lax.all_to_all(values, 'seq', split_axis=0, concat_axis=1, tiled=True)  10.5 us
    unnamed x15, local copies, waits for them, and re-layouts  9.92 us
    dot_general x1, matrix products, body(): gate_sum = jnp.dot(tokens, full_weight, preferred_element_type=jnp.float32)  8.14 us
  transfers between devices with their start and end apart: 5, of which 4 were waited for; matrix products, arithmetic and copies ran while one was open for 10% of the time, Pallas kernels for 0%

commit v1 on v0

--- a/solution.py
+++ b/solution.py
@@ -1,6 +1,10 @@
+import functools
+
 import jax
 import jax.numpy as jnp
 from jax import lax
+from jax.experimental import pallas as pl
+from jax.experimental.pallas import tpu as pltpu
 from jax.sharding import PartitionSpec as P
 
 
@@ -69,6 +73,322 @@
     return (output.reshape(tok_rows, channels), input_grad, gate_grad, left_grad, right_grad)
 
 
+F32 = jnp.float32
+BF16 = jnp.bfloat16
+ROWS = 16
+PLANE = 4
+
+
+def mixer_kernel(
+    n, tok, cot, wsh, left, rk,
+    out, igrad, ggrad, lgrad, rgrad,
+    wf, first_s, sg_s, fc, gc, sc, fgc, sr, fr, gate, delta, part, wt, half, quarter, tail, mix,
+    ssem, rsem, ws_sem, wr_sem, gs_sem, gr_sem,
+):
+    me = lax.axis_index("seq")
+    zi, qi = me // PLANE, me % PLANE
+    chunks = fc.shape[0]
+    blocks, width = tok.shape[0], tok.shape[2]
+    nz = n // PLANE
+    deep = fc.shape[1] * ROWS
+    tile = 256
+    per = tile // ROWS
+    row_tiles = tok.shape[1] // tile
+
+    barrier = pltpu.get_barrier_semaphore()
+
+    def greet(s, carry):
+        pl.semaphore_signal(barrier, inc=1, device_id={"seq": (me + s) % n}, device_id_type=pl.DeviceIdType.MESH)
+        return carry
+
+    lax.fori_loop(1, n, greet, 0)
+    pl.semaphore_wait(barrier, n - 1)
+
+    def remote(src, dst, ss, rs, dev):
+        return pltpu.make_async_remote_copy(
+            src_ref=src, dst_ref=dst, send_sem=ss, recv_sem=rs,
+            device_id={"seq": dev}, device_id_type=pl.DeviceIdType.MESH,
+        )
+
+    def to_cols(ph, k, src, dst, s):
+        t = (s * 7) % n
+        peer = (me + t) % n
+        return remote(
+            src.at[:, peer * chunks + k], dst.at[k, pl.ds(me * blocks, blocks)],
+            ssem.at[ph, k, t], rsem.at[ph, k, t], peer,
+        )
+
+    def to_rows_(ph, k, src, dst, s):
+        t = (s * 7) % n
+        peer = (me + t) % n
+        return remote(
+            src.at[k, pl.ds(peer * blocks, blocks)], dst.at[:, me * chunks + k],
+            ssem.at[ph, k, t], rsem.at[ph, k, t], peer,
+        )
+
+    def each(make, action):
+        def step(s, carry):
+            copy = make(s)
+            if action == "start":
+                copy.start()
+            elif action == "recv":
+                copy.wait_recv()
+            else:
+                copy.wait_send()
+            return carry
+
+        lax.fori_loop(1, n, step, 0)
+
+    def w_z(d):
+        return remote(wsh, wf.at[zi, qi], ws_sem.at[0, d], wr_sem.at[0, d], ((zi + d) % nz) * PLANE + qi)
+
+    def w_q(d):
+        return remote(wf.at[:, qi], wf.at[:, qi], ws_sem.at[1, d], wr_sem.at[1, d], zi * PLANE + (qi + d) % PLANE)
+
+    for d in range(1, nz):
+        w_z(d).start()
+    wf[zi, qi] = wsh[...]
+
+    def first_tile(t, carry):
+        a, j = t // row_tiles, t % row_tiles
+        prod = jnp.dot(left[a, pl.ds(j * tile, tile), :], tok[a], preferred_element_type=F32)
+        first_s[a, pl.ds(j * per, per)] = prod.astype(BF16).reshape(per, ROWS, width)
+        return carry
+
+    lax.fori_loop(0, blocks * row_tiles, first_tile, 0)
+    for d in range(1, nz):
+        w_z(d).wait_recv()
+    for d in range(1, PLANE):
+        w_q(d).start()
+    for k in range(chunks):
+        each(functools.partial(to_cols, 0, k, first_s, fc), "start")
+        fc[k, pl.ds(me * blocks, blocks)] = first_s[:, me * chunks + k]
+
+    spread = (
+        lax.broadcasted_iota(jnp.int32, (deep // ROWS, deep), 1) // ROWS
+        == lax.broadcasted_iota(jnp.int32, (deep // ROWS, deep), 0)
+    ).astype(F32).astype(BF16)
+    same = (
+        lax.broadcasted_iota(jnp.int32, (deep, deep), 0) % ROWS
+        == lax.broadcasted_iota(jnp.int32, (deep, deep), 1) % ROWS
+    )
+    for k in range(chunks):
+        wide = jnp.dot(rk[k], spread, preferred_element_type=F32)
+        mix[k] = jnp.where(same, wide, 0.0).astype(BF16)
+
+    for d in range(1, PLANE):
+        w_q(d).wait_recv()
+
+    def gate_tile(t, carry):
+        a, j = t // row_tiles, t % row_tiles
+        rows = pl.ds(j * tile, tile)
+        weight = wf[...].reshape(width, width)
+        g = jnp.dot(tok[a, rows, :], weight, preferred_element_type=F32).astype(BF16)
+        gate[a, rows, :] = g
+        gf = g.astype(F32)
+        up = cot[a, rows, :].astype(F32) * (gf * jax.nn.sigmoid(gf))
+        sg_s[a, pl.ds(j * per, per)] = up.astype(BF16).reshape(per, ROWS, width)
+        return carry
+
+    lax.fori_loop(0, blocks * row_tiles, gate_tile, 0)
+    for k in range(chunks):
+        each(functools.partial(to_cols, 1, k, sg_s, gc), "start")
+        gc[k, pl.ds(me * blocks, blocks)] = sg_s[:, me * chunks + k]
+
+    def mixed(k, src, dst, dims):
+        def step(t, carry):
+            cols = pl.ds(pl.multiple_of(t * tile, tile), tile)
+            x = src[k, :, :, cols].reshape(deep, tile)
+            y = lax.dot_general(mix[k], x, (dims, ((), ())), preferred_element_type=F32)
+            dst[k, :, :, cols] = y.astype(BF16).reshape(deep // ROWS, ROWS, tile)
+            return carry
+
+        lax.fori_loop(0, width // tile, step, 0)
+
+    for k in range(chunks):
+        each(functools.partial(to_cols, 0, k, first_s, fc), "recv")
+        mixed(k, fc, sc, ((1,), (0,)))
+        each(functools.partial(to_rows_, 2, k, sc, sr), "start")
+        sr[:, me * chunks + k] = sc[k, pl.ds(me * blocks, blocks)]
+    for k in range(chunks):
+        each(functools.partial(to_cols, 1, k, sg_s, gc), "recv")
+        mixed(k, gc, fgc, ((0,), (0,)))
+        each(functools.partial(to_rows_, 3, k, fgc, fr), "start")
+        fr[:, me * chunks + k] = fgc[k, pl.ds(me * blocks, blocks)]
+
+    scale_w = width ** (-0.5)
+    for k in range(chunks):
+        pairs = lax.dot_general(
+            gc[k].reshape(deep, width), fc[k].reshape(deep, width),
+            (((1,), (1,)), ((), ())), preferred_element_type=F32,
+        )
+        kept = jnp.where(same, pairs * scale_w, 0.0).astype(BF16)
+        rgrad[k] = lax.dot_general(
+            kept, spread, (((1,), (1,)), ((), ())), preferred_element_type=F32
+        ).astype(BF16)
+
+    for k in range(chunks):
+        each(functools.partial(to_rows_, 2, k, sc, sr), "recv")
+
+    def delta_tile(t, carry):
+        a, j = t // row_tiles, t % row_tiles
+        rows = pl.ds(j * tile, tile)
+        gf = gate[a, rows, :].astype(F32)
+        sig = jax.nn.sigmoid(gf)
+        sec = sr[a, pl.ds(j * per, per)].reshape(tile, width).astype(F32)
+        up = cot[a, rows, :].astype(F32)
+        out[a, rows, :] = (sec * (gf * sig)).astype(BF16)
+        delta[a, rows, :] = (up * sec * (sig * (1.0 + gf * (1.0 - sig)))).astype(BF16)
+        return carry
+
+    lax.fori_loop(0, blocks * row_tiles, delta_tile, 0)
+
+    def weight_tile(z, carry):
+        cols = pl.ds(pl.multiple_of(z * tile, tile), tile)
+        tokens_2d = tok[:, :, cols].reshape(blocks * tok.shape[1], tile)
+        delta_2d = delta[...].reshape(blocks * tok.shape[1], width)
+        prod = lax.dot_general(tokens_2d, delta_2d, (((0,), (0,)), ((), ())), preferred_element_type=F32)
+        wt[z] = prod.astype(BF16).reshape(PLANE, tile // PLANE, width)
+        return carry
+
+    lax.fori_loop(0, width // tile, weight_tile, 0)
+
+    def g_q(d):
+        peer = (qi + d) % PLANE
+        return remote(wt.at[:, peer], half.at[d - 1], gs_sem.at[0, d], gr_sem.at[0, d], zi * PLANE + peer)
+
+    def g_z(d):
+        peer = (zi + d) % nz
+        return remote(quarter.at[peer], tail.at[d - 1], gs_sem.at[1, d], gr_sem.at[1, d], peer * PLANE + qi)
+
+    for d in range(1, PLANE):
+        g_q(d).start()
+
+    def part_tile(t, carry):
+        a, j = t // row_tiles, t % row_tiles
+        rows = pl.ds(j * tile, tile)
+        weight = wf[...].reshape(width, width)
+        part[a, rows, :] = lax.dot_general(
+            delta[a, rows, :], weight, (((1,), (1,)), ((), ())), preferred_element_type=F32
+        )
+        return carry
+
+    lax.fori_loop(0, blocks * row_tiles, part_tile, 0)
+
+    for d in range(1, PLANE):
+        g_q(d).wait_recv()
+
+    def sum_tile(z, carry):
+        total = wt[z, qi].astype(F32)
+        for d in range(PLANE - 1):
+            total = total + half[d, z].astype(F32)
+        quarter[z] = total.astype(BF16)
+        return carry
+
+    lax.fori_loop(0, nz, sum_tile, 0)
+    for d in range(1, nz):
+        g_z(d).start()
+    for d in range(1, nz):
+        g_z(d).wait_recv()
+    total = quarter[zi].astype(F32)
+    for d in range(nz - 1):
+        total = total + tail[d].astype(F32)
+    ggrad[...] = total * (blocks * tok.shape[1] * n) ** (-0.5)
+
+    for k in range(chunks):
+        each(functools.partial(to_rows_, 3, k, fgc, fr), "recv")
+
+    def last_tile(t, carry):
+        a, j = t // row_tiles, t % row_tiles
+        rows = pl.ds(pl.multiple_of(j * tile, tile), tile)
+        lg = lax.dot_general(
+            fr[a, pl.ds(j * per, per)].reshape(tile, width), tok[a],
+            (((1,), (1,)), ((), ())), preferred_element_type=F32,
+        )
+        lgrad[a, rows, :] = (lg * scale_w).astype(BF16)
+        mixer = lax.dot_general(
+            left[a, :, rows], fr[a].reshape(tok.shape[1], width),
+            (((0,), (0,)), ((), ())), preferred_element_type=F32,
+        )
+        igrad[a, rows, :] = (mixer + part[a, rows, :]).astype(BF16)
+        return carry
+
+    lax.fori_loop(0, blocks * row_tiles, last_tile, 0)
+
+    for k in range(chunks):
+        each(functools.partial(to_cols, 0, k, first_s, fc), "send")
+        each(functools.partial(to_cols, 1, k, sg_s, gc), "send")
+        each(functools.partial(to_rows_, 2, k, sc, sr), "send")
+        each(functools.partial(to_rows_, 3, k, fgc, fr), "send")
+    for d in range(1, nz):
+        w_z(d).wait_send()
+        g_z(d).wait_send()
+    for d in range(1, PLANE):
+        w_q(d).wait_send()
+        g_q(d).wait_send()
+
+
+def fused_body(n, tokens, cotangent, gate_weight, left_blocks, right_blocks):
+    blocks, inner = left_blocks.shape[0], left_blocks.shape[1]
+    own, outer = right_blocks.shape[0], right_blocks.shape[1]
+    width = tokens.shape[1]
+    chunks = own // ROWS
+    groups = inner // ROWS
+    deep = outer * ROWS
+    nz = n // PLANE
+    shard = width // n
+    rk = right_blocks.reshape(chunks, ROWS, outer, outer).transpose(0, 2, 1, 3).reshape(chunks, deep, outer)
+    rows = (blocks, inner, width)
+    by_row = pltpu.VMEM((blocks, groups, ROWS, width), BF16)
+    by_col = pltpu.VMEM((chunks, outer, ROWS, width), BF16)
+    vmem = pl.BlockSpec(memory_space=pltpu.VMEM)
+    out, igrad, ggrad, lgrad, rgrad = pl.pallas_call(
+        functools.partial(mixer_kernel, n),
+        out_shape=(
+            jax.ShapeDtypeStruct(rows, BF16),
+            jax.ShapeDtypeStruct(rows, BF16),
+            jax.ShapeDtypeStruct((shard, width), F32),
+            jax.ShapeDtypeStruct((blocks, inner, inner), BF16),
+            jax.ShapeDtypeStruct((chunks, deep, outer), BF16),
+        ),
+        in_specs=[vmem] * 5,
+        out_specs=[vmem] * 5,
+        scratch_shapes=[
+            pltpu.VMEM((nz, PLANE, shard, width), BF16),
+            by_row, by_row, by_col, by_col, by_col, by_col, by_row, by_row,
+            pltpu.VMEM(rows, BF16),
+            pltpu.VMEM(rows, BF16),
+            pltpu.VMEM(rows, F32),
+            pltpu.VMEM((nz, PLANE, shard, width), BF16),
+            pltpu.VMEM((PLANE - 1, nz, shard, width), BF16),
+            pltpu.VMEM((nz, shard, width), BF16),
+            pltpu.VMEM((nz - 1, shard, width), BF16),
+            pltpu.VMEM((chunks, deep, deep), BF16),
+            pltpu.SemaphoreType.DMA((4, chunks, n)),
+            pltpu.SemaphoreType.DMA((4, chunks, n)),
+            pltpu.SemaphoreType.DMA((2, PLANE)),
+            pltpu.SemaphoreType.DMA((2, PLANE)),
+            pltpu.SemaphoreType.DMA((2, PLANE)),
+            pltpu.SemaphoreType.DMA((2, PLANE)),
+        ],
+        compiler_params=pltpu.CompilerParams(
+            collective_id=0, has_side_effects=True, vmem_limit_bytes=60 * 2**20
+        ),
+    )(
+        tokens.reshape(rows), cotangent.reshape(rows), gate_weight, left_blocks, rk
+    )
+    rgrad = rgrad.reshape(chunks, outer, ROWS, outer).transpose(0, 2, 1, 3).reshape(own, outer, outer)
+    return (out.reshape(tokens.shape), igrad.reshape(tokens.shape), ggrad, lgrad, rgrad)
+
+
+def chosen_body(tokens, cotangent, gate_weight, left_blocks, right_blocks):
+    n = lax.axis_size("seq")
+    own, width, inner = right_blocks.shape[0], tokens.shape[1], left_blocks.shape[1]
+    if n == PLANE * PLANE and own % ROWS == 0 and width == 256 * PLANE and inner % 256 == 0:
+        return fused_body(n, tokens, cotangent, gate_weight, left_blocks, right_blocks)
+    return body(tokens, cotangent, gate_weight, left_blocks, right_blocks)
+
+
 def solution(mesh):
     in_specs = (
         P(("groups", "seq"), None),
@@ -84,4 +404,4 @@
         P(("groups", "seq"), None, None),
         P(("groups", "seq"), None, None),
     )
-    return jax.shard_map(body, mesh=mesh, in_specs=in_specs, out_specs=out_specs, check_vma=False)
+    return jax.shard_map(chosen_body, mesh=mesh, in_specs=in_specs, out_specs=out_specs, check_vma=False)

time: 314 us -> 237 us (0.75)
  Pallas kernels: 0 us -> 227 us
  waiting for transfers between devices: 152 us -> 0 us
  blocking collectives: 53.7 us -> 0 us
  local copies, waits for them, and re-layouts: 43.4 us -> 9.75 us
  matrix products: 32.2 us -> 0 us
  starting transfers between devices: 15.9 us -> 0 us
  between operations: 14.1 us -> 0.64 us
    pallas_call x0 -> x1, Pallas kernels: none -> 227 us  [fused_body(): pl.pallas_call(functools.partial(mixer_kernel, n), out_shape=(jax.ShapeDt...]
    all_to_all x3 -> x0, waiting for transfers between devices: 133 us -> none  [the longest x2 89 us: to_rows(): lax.all_to_all(values, 'seq', split_axis=0, concat_axis=1, tiled=True)]
    all_to_all x1 -> x0, blocking collectives: 53.7 us -> none  [to_columns(): lax.all_to_all(values, 'seq', split_axis=1, concat_axis=0, tiled=True)]
    dot_general x9 -> x0, matrix products: 32.2 us -> none  [the longest x1 8.14 us: body(): gate_sum = jnp.dot(tokens, full_weight, preferred_element_type=jnp.float32)]
    unnamed x3 -> x0, waiting for transfers between devices: 18.9 us -> none
    all_to_all x5 -> x0, local copies, waits for them, and re-layouts: 18.8 us -> none  [the longest x4 17 us: to_columns(): lax.all_to_all(values, 'seq', split_axis=1, concat_axis=0, tiled=True)]
    all_to_all x3 -> x0, starting transfers between devices: 15.4 us -> none  [the longest x2 10.5 us: to_rows(): lax.all_to_all(values, 'seq', split_axis=0, concat_axis=1, tiled=True)]
    convert_element_type x5 -> x0, local copies, waits for them, and re-layouts: 14.6 us -> none  [the longest x1 4.05 us: body(): second_f = second.astype(jnp.float32)]
  transfers between devices with their start and end apart: 5 -> 0, of which waited for: 4 -> 0; matrix products, arithmetic and copies ran while one was open for 10% -> 0% of each run, Pallas kernels for 0% -> 0%
where the time goes in v1:
time: 237 us
  Pallas kernels  227 us (96%)
  local copies, waits for them, and re-layouts  9.75 us (4%)
    pallas_call x1, Pallas kernels, fused_body(): pl.pallas_call(functools.partial(mixer_kernel, n), out_shape=(jax.ShapeDt...  227 us
    unnamed x10, local copies, waits for them, and re-layouts  6.27 us

profile of v1, /device:TPU:13, one launch (start us, length us, event | category | flops | bytes accessed | tf_op | source)
XLA Modules:
  0.0 237.2 jit_solution(5581673852408985617)
XLA Ops:
  0.6 1.8 copy.10
  2.4 226.8 %shard_map.92 = (bf16[2,512,1024]{2,1,0:T(8,128)(2,1)}, bf16[2,512,1024]{2,1,0:T(8,128)(2,1)}, f32[64,1024]{1,0:T(8,128)}, bf16[2,512,512]{2,1,0:T(8,128)(2,1)}, bf16[2,512,32]{2,1,0:T(8,128)(2,1)}) custom-call(bf16[2,512,1024]{2,1,0:T(8,128)(2,1)} %bitcast.14, bf16[2,512,1024]{2,1,0:T(8,128)(2,1)} %bitcast.15, bf16[64,1024]{1,0:T(8,128)(2,1)} %wsh.1, ...), custom_call_target="tpu_custom_call" | custom-call | tf_op jit(solution)/shard_map/pallas_call | solution.py:345
  229.2 1.7 copy.11
  230.9 0.0 copy-start
  230.9 3.2 %copy.16 = bf16[1024,1024]{1,0:T(8,128)(2,1)} copy(bf16[1024,1024]{1,0:T(8,128)(2,1)} %bitcast.13) | data formatting | bytes 4194304
  234.1 0.0 copy-done
  234.1 0.0 copy-start.2
  234.1 0.0 copy-start.1
  234.1 1.3 copy.17
  235.5 0.0 copy-done.2
  235.5 0.7 copy.18
  236.2 0.0 copy-done.1
  236.2 1.0 copy.19
Async XLA Ops:
  230.9 3.2 %copy-start = (bf16[2,512,1024]{2,1,0:T(8,128)(2,1)S(1)}, bf16[2,512,1024]{2,1,0:T(8,128)(2,1)}, u32[]{:S(2)}) copy-start(bf16[2,512,1024]{2,1,0:T(8,128)(2,1)} %get-tuple-element.11) | copy-start | bytes 6291460
  234.1 1.3 copy-start.2
  234.1 2.1 copy-start.1

commit v2 on v1

--- a/solution.py
+++ b/solution.py
@@ -80,10 +80,10 @@
 
 
 def mixer_kernel(
-    n, tok, cot, wsh, left, rk,
-    out, igrad, ggrad, lgrad, rgrad,
-    wf, first_s, sg_s, fc, gc, sc, fgc, sr, fr, gate, delta, part, wt, half, quarter, tail, mix,
-    ssem, rsem, ws_sem, wr_sem, gs_sem, gr_sem,
+    n, tok_hbm, cot_hbm, wsh, left_hbm, right,
+    out_hbm, part_hbm, fr, ggrad, rgrad,
+    tok, cot, left, out, part, wf, first_s, sg_s, fc, gc, sc, fgc, sr, gate, delta, wt, half, quarter, pair, tail, mix,
+    ssem, rsem, ws_sem, wr_sem, gs_sem, gr_sem, lsem,
 ):
     me = lax.axis_index("seq")
     zi, qi = me // PLANE, me % PLANE
@@ -95,6 +95,15 @@
     per = tile // ROWS
     row_tiles = tok.shape[1] // tile
 
+    loads = [
+        pltpu.make_async_copy(left_hbm, left, lsem.at[0]),
+        pltpu.make_async_copy(tok_hbm, tok, lsem.at[1]),
+        pltpu.make_async_copy(wsh, wf.at[zi, qi], lsem.at[2]),
+        pltpu.make_async_copy(cot_hbm, cot, lsem.at[3]),
+    ]
+    for load in loads:
+        load.start()
+
     barrier = pltpu.get_barrier_semaphore()
 
     def greet(s, carry):
@@ -139,15 +148,20 @@
 
         lax.fori_loop(1, n, step, 0)
 
-    def w_z(d):
-        return remote(wsh, wf.at[zi, qi], ws_sem.at[0, d], wr_sem.at[0, d], ((zi + d) % nz) * PLANE + qi)
+    across = (zi + nz // 2) % nz
+    beside = zi + 1 - 2 * (zi % 2)
+
+    w_far = remote(wsh, wf.at[zi, qi], ws_sem.at[0, 0], wr_sem.at[0, 0], across * PLANE + qi)
+    w_near = remote(wsh, wf.at[zi, qi], ws_sem.at[0, 1], wr_sem.at[0, 1], beside * PLANE + qi)
+    w_pass = remote(wf.at[across, qi], wf.at[across, qi], ws_sem.at[0, 2], wr_sem.at[0, 2], beside * PLANE + qi)
 
     def w_q(d):
         return remote(wf.at[:, qi], wf.at[:, qi], ws_sem.at[1, d], wr_sem.at[1, d], zi * PLANE + (qi + d) % PLANE)
 
-    for d in range(1, nz):
-        w_z(d).start()
-    wf[zi, qi] = wsh[...]
+    w_far.start()
+    w_near.start()
+    loads[0].wait()
+    loads[1].wait()
 
     def first_tile(t, carry):
         a, j = t // row_tiles, t % row_tiles
@@ -156,11 +170,15 @@
         return carry
 
     lax.fori_loop(0, blocks * row_tiles, first_tile, 0)
-    for d in range(1, nz):
-        w_z(d).wait_recv()
-    for d in range(1, PLANE):
-        w_q(d).start()
-    for k in range(chunks):
+    w_far.wait_recv()
+    w_pass.start()
+    for k in range(chunks):
+        if k == 1:
+            loads[2].wait()
+            w_near.wait_recv()
+            w_pass.wait_recv()
+            for d in range(1, PLANE):
+                w_q(d).start()
         each(functools.partial(to_cols, 0, k, first_s, fc), "start")
         fc[k, pl.ds(me * blocks, blocks)] = first_s[:, me * chunks + k]
 
@@ -172,12 +190,18 @@
         lax.broadcasted_iota(jnp.int32, (deep, deep), 0) % ROWS
         == lax.broadcasted_iota(jnp.int32, (deep, deep), 1) % ROWS
     )
-    for k in range(chunks):
-        wide = jnp.dot(rk[k], spread, preferred_element_type=F32)
+    outer = deep // ROWS
+    row = lax.broadcasted_iota(jnp.int32, (deep, deep), 0)
+    col = lax.broadcasted_iota(jnp.int32, (deep, deep), 1)
+    turn = ((row // ROWS == col % outer) & (row % ROWS == col // outer)).astype(F32).astype(BF16)
+    for k in range(chunks):
+        rk = jnp.dot(turn, right[k], preferred_element_type=F32).astype(BF16)
+        wide = jnp.dot(rk, spread, preferred_element_type=F32)
         mix[k] = jnp.where(same, wide, 0.0).astype(BF16)
 
     for d in range(1, PLANE):
         w_q(d).wait_recv()
+    loads[3].wait()
 
     def gate_tile(t, carry):
         a, j = t // row_tiles, t % row_tiles
@@ -214,7 +238,9 @@
         each(functools.partial(to_cols, 1, k, sg_s, gc), "recv")
         mixed(k, gc, fgc, ((0,), (0,)))
         each(functools.partial(to_rows_, 3, k, fgc, fr), "start")
-        fr[:, me * chunks + k] = fgc[k, pl.ds(me * blocks, blocks)]
+        pltpu.make_async_copy(
+            fgc.at[k, pl.ds(me * blocks, blocks)], fr.at[:, me * chunks + k], lsem.at[4 + k]
+        ).start()
 
     scale_w = width ** (-0.5)
     for k in range(chunks):
@@ -223,8 +249,11 @@
             (((1,), (1,)), ((), ())), preferred_element_type=F32,
         )
         kept = jnp.where(same, pairs * scale_w, 0.0).astype(BF16)
+        picked = lax.dot_general(
+            kept, spread, (((1,), (1,)), ((), ())), preferred_element_type=F32
+        ).astype(BF16)
         rgrad[k] = lax.dot_general(
-            kept, spread, (((1,), (1,)), ((), ())), preferred_element_type=F32
+            turn, picked, (((0,), (0,)), ((), ())), preferred_element_type=F32
         ).astype(BF16)
 
     for k in range(chunks):
@@ -242,6 +271,8 @@
         return carry
 
     lax.fori_loop(0, blocks * row_tiles, delta_tile, 0)
+    out_copy = pltpu.make_async_copy(out, out_hbm, lsem.at[0])
+    out_copy.start()
 
     def weight_tile(z, carry):
         cols = pl.ds(pl.multiple_of(z * tile, tile), tile)
@@ -257,9 +288,13 @@
         peer = (qi + d) % PLANE
         return remote(wt.at[:, peer], half.at[d - 1], gs_sem.at[0, d], gr_sem.at[0, d], zi * PLANE + peer)
 
-    def g_z(d):
-        peer = (zi + d) % nz
-        return remote(quarter.at[peer], tail.at[d - 1], gs_sem.at[1, d], gr_sem.at[1, d], peer * PLANE + qi)
+    g_near = [
+        remote(quarter.at[beside], tail.at[0], gs_sem.at[1, 0], gr_sem.at[1, 0], beside * PLANE + qi),
+        remote(
+            quarter.at[(beside + nz // 2) % nz], tail.at[1], gs_sem.at[1, 1], gr_sem.at[1, 1], beside * PLANE + qi
+        ),
+    ]
+    g_far = remote(pair, tail.at[2], gs_sem.at[1, 2], gr_sem.at[1, 2], across * PLANE + qi)
 
     for d in range(1, PLANE):
         g_q(d).start()
@@ -270,10 +305,12 @@
         weight = wf[...].reshape(width, width)
         part[a, rows, :] = lax.dot_general(
             delta[a, rows, :], weight, (((1,), (1,)), ((), ())), preferred_element_type=F32
-        )
+        ).astype(BF16)
         return carry
 
     lax.fori_loop(0, blocks * row_tiles, part_tile, 0)
+    part_copy = pltpu.make_async_copy(part, part_hbm, lsem.at[1])
+    part_copy.start()
 
     for d in range(1, PLANE):
         g_q(d).wait_recv()
@@ -286,46 +323,46 @@
         return carry
 
     lax.fori_loop(0, nz, sum_tile, 0)
-    for d in range(1, nz):
-        g_z(d).start()
-    for d in range(1, nz):
-        g_z(d).wait_recv()
-    total = quarter[zi].astype(F32)
-    for d in range(nz - 1):
-        total = total + tail[d].astype(F32)
+    for copy in g_near:
+        copy.start()
+    for copy in g_near:
+        copy.wait_recv()
+    pair[...] = (quarter[across].astype(F32) + tail[1].astype(F32)).astype(BF16)
+    g_far.start()
+    g_far.wait_recv()
+    total = quarter[zi].astype(F32) + tail[0].astype(F32) + tail[2].astype(F32)
     ggrad[...] = total * (blocks * tok.shape[1] * n) ** (-0.5)
 
     for k in range(chunks):
         each(functools.partial(to_rows_, 3, k, fgc, fr), "recv")
-
-    def last_tile(t, carry):
-        a, j = t // row_tiles, t % row_tiles
-        rows = pl.ds(pl.multiple_of(j * tile, tile), tile)
-        lg = lax.dot_general(
-            fr[a, pl.ds(j * per, per)].reshape(tile, width), tok[a],
-            (((1,), (1,)), ((), ())), preferred_element_type=F32,
-        )
-        lgrad[a, rows, :] = (lg * scale_w).astype(BF16)
-        mixer = lax.dot_general(
-            left[a, :, rows], fr[a].reshape(tok.shape[1], width),
-            (((0,), (0,)), ((), ())), preferred_element_type=F32,
-        )
-        igrad[a, rows, :] = (mixer + part[a, rows, :]).astype(BF16)
-        return carry
-
-    lax.fori_loop(0, blocks * row_tiles, last_tile, 0)
+        pltpu.make_async_copy(
+            fgc.at[k, pl.ds(me * blocks, blocks)], fr.at[:, me * chunks + k], lsem.at[4 + k]
+        ).wait()
+    out_copy.wait()
+    part_copy.wait()
 
     for k in range(chunks):
         each(functools.partial(to_cols, 0, k, first_s, fc), "send")
         each(functools.partial(to_cols, 1, k, sg_s, gc), "send")
         each(functools.partial(to_rows_, 2, k, sc, sr), "send")
         each(functools.partial(to_rows_, 3, k, fgc, fr), "send")
-    for d in range(1, nz):
-        w_z(d).wait_send()
-        g_z(d).wait_send()
+    for copy in (w_far, w_near, w_pass, *g_near, g_far):
+        copy.wait_send()
     for d in range(1, PLANE):
         w_q(d).wait_send()
         g_q(d).wait_send()
+
+
+def last_kernel(scale_w, tok, left, fr, part, out_in, ggrad_in, rgrad_in, out, igrad, lgrad, ggrad, rgrad):
+    size = part.shape[1]
+    rows = pl.ds(pl.multiple_of((pl.program_id(0) % (tok.shape[1] // size)) * size, size), size)
+    out[...] = out_in[...]
+    ggrad[...] = ggrad_in[...]
+    rgrad[...] = rgrad_in[...]
+    lg = lax.dot_general(fr[0, rows, :], tok[0], (((1,), (1,)), ((), ())), preferred_element_type=F32)
+    lgrad[0] = (lg * scale_w).astype(BF16)
+    mixer = lax.dot_general(left[0], fr[0], (((0,), (0,)), ((), ())), preferred_element_type=F32)
+    igrad[0] = (mixer + part[0].astype(F32)).astype(BF16)
 
 
 def fused_body(n, tokens, cotangent, gate_weight, left_blocks, right_blocks):
@@ -337,32 +374,38 @@
     deep = outer * ROWS
     nz = n // PLANE
     shard = width // n
-    rk = right_blocks.reshape(chunks, ROWS, outer, outer).transpose(0, 2, 1, 3).reshape(chunks, deep, outer)
     rows = (blocks, inner, width)
     by_row = pltpu.VMEM((blocks, groups, ROWS, width), BF16)
     by_col = pltpu.VMEM((chunks, outer, ROWS, width), BF16)
     vmem = pl.BlockSpec(memory_space=pltpu.VMEM)
-    out, igrad, ggrad, lgrad, rgrad = pl.pallas_call(
+    hbm = pl.BlockSpec(memory_space=pltpu.HBM)
+    token_grid = tokens.reshape(rows)
+    out, part, fr, ggrad, rgrad = pl.pallas_call(
         functools.partial(mixer_kernel, n),
         out_shape=(
             jax.ShapeDtypeStruct(rows, BF16),
             jax.ShapeDtypeStruct(rows, BF16),
+            jax.ShapeDtypeStruct((blocks, groups, ROWS, width), BF16),
             jax.ShapeDtypeStruct((shard, width), F32),
-            jax.ShapeDtypeStruct((blocks, inner, inner), BF16),
             jax.ShapeDtypeStruct((chunks, deep, outer), BF16),
         ),
-        in_specs=[vmem] * 5,
-        out_specs=[vmem] * 5,
+        in_specs=[hbm, hbm, hbm, hbm, vmem],
+        out_specs=[hbm, hbm, hbm, vmem, vmem],
         scratch_shapes=[
+            pltpu.VMEM(rows, BF16),
+            pltpu.VMEM(rows, BF16),
+            pltpu.VMEM((blocks, inner, inner), BF16),
+            pltpu.VMEM(rows, BF16),
+            pltpu.VMEM(rows, BF16),
             pltpu.VMEM((nz, PLANE, shard, width), BF16),
-            by_row, by_row, by_col, by_col, by_col, by_col, by_row, by_row,
-            pltpu.VMEM(rows, BF16),
-            pltpu.VMEM(rows, BF16),
-            pltpu.VMEM(rows, F32),
+            by_row, by_row, by_col, by_col, by_col, by_col, by_row,
+            pltpu.VMEM(rows, BF16),
+            pltpu.VMEM(rows, BF16),
             pltpu.VMEM((nz, PLANE, shard, width), BF16),
             pltpu.VMEM((PLANE - 1, nz, shard, width), BF16),
             pltpu.VMEM((nz, shard, width), BF16),
-            pltpu.VMEM((nz - 1, shard, width), BF16),
+            pltpu.VMEM((shard, width), BF16),
+            pltpu.VMEM((3, shard, width), BF16),
             pltpu.VMEM((chunks, deep, deep), BF16),
             pltpu.SemaphoreType.DMA((4, chunks, n)),
             pltpu.SemaphoreType.DMA((4, chunks, n)),
@@ -370,14 +413,37 @@
             pltpu.SemaphoreType.DMA((2, PLANE)),
             pltpu.SemaphoreType.DMA((2, PLANE)),
             pltpu.SemaphoreType.DMA((2, PLANE)),
+            pltpu.SemaphoreType.DMA((4 + chunks,)),
         ],
         compiler_params=pltpu.CompilerParams(
             collective_id=0, has_side_effects=True, vmem_limit_bytes=60 * 2**20
         ),
     )(
-        tokens.reshape(rows), cotangent.reshape(rows), gate_weight, left_blocks, rk
+        token_grid, cotangent.reshape(rows), gate_weight, left_blocks, right_blocks.reshape(chunks, deep, outer)
     )
-    rgrad = rgrad.reshape(chunks, outer, ROWS, outer).transpose(0, 2, 1, 3).reshape(own, outer, outer)
+    size = 256
+    per_block = inner // size
+    steps = blocks * per_block
+    tall = pl.BlockSpec((1, inner, width), lambda t: (t // per_block, 0, 0))
+    flat = pl.BlockSpec((1, size, width), lambda t: (t // per_block, t % per_block, 0))
+    square = pl.BlockSpec((1, size, inner), lambda t: (t // per_block, t % per_block, 0))
+    side = pl.BlockSpec((1, inner, size), lambda t: (t // per_block, 0, t % per_block))
+    weight_spec = pl.BlockSpec((shard // steps, width), lambda t: (t, 0))
+    right_spec = pl.BlockSpec((own * outer // steps, outer), lambda t: (t, 0))
+    out, igrad, lgrad, ggrad, rgrad = pl.pallas_call(
+        functools.partial(last_kernel, width ** (-0.5)),
+        grid=(steps,),
+        out_shape=(
+            jax.ShapeDtypeStruct(rows, BF16),
+            jax.ShapeDtypeStruct(rows, BF16),
+            jax.ShapeDtypeStruct((blocks, inner, inner), BF16),
+            jax.ShapeDtypeStruct((shard, width), F32),
+            jax.ShapeDtypeStruct((own * outer, outer), BF16),
+        ),
+        in_specs=[tall, side, tall, flat, flat, weight_spec, right_spec],
+        out_specs=[flat, flat, square, weight_spec, right_spec],
+    )(token_grid, left_blocks, fr.reshape(rows), part, out, ggrad, rgrad.reshape(own * outer, outer))
+    rgrad = rgrad.reshape(own, outer, outer)
     return (out.reshape(tokens.shape), igrad.reshape(tokens.shape), ggrad, lgrad, rgrad)
 
 

time: 237 us -> 228 us (0.962); the launches traced: 237 us -> 225 us
  local copies, waits for them, and re-layouts: 9.75 us -> 0 us
    pallas_call x1, Pallas kernels: 227 us -> 216 us  [fused_body(): pl.pallas_call(functools.partial(mixer_kernel, n), out_shape=(jax.ShapeDt...]
    pallas_call x0 -> x1, Pallas kernels: none -> 8.31 us  [fused_body(): pl.pallas_call(functools.partial(last_kernel, width ** (-0.5)), grid=(ste...]
    unnamed x10 -> x0, local copies, waits for them, and re-layouts: 6.27 us -> none
where the time goes in v2:
time: 228 us; the launch traced here: 225 us
  Pallas kernels  225 us (99%)
    pallas_call x1, Pallas kernels, fused_body(): pl.pallas_call(functools.partial(mixer_kernel, n), out_shape=(jax.ShapeDt...  216 us
    pallas_call x1, Pallas kernels, fused_body(): pl.pallas_call(functools.partial(last_kernel, width ** (-0.5)), grid=(ste...  8.31 us

profile of v2, /device:TPU:13, one launch (start us, length us, event | category | flops | bytes accessed | tf_op | source)
XLA Modules:
  0.0 225.4 jit_solution(7192487988328133838)
XLA Ops:
  0.6 216.4 %shard_map.92 = (bf16[2,512,1024]{2,1,0:T(8,128)(2,1)}, bf16[2,512,1024]{2,1,0:T(8,128)(2,1)}, bf16[2,32,16,1024]{3,2,1,0:T(8,128)(2,1)}, f32[64,1024]{1,0:T(8,128)}, bf16[2,512,32]{2,1,0:T(8,128)(2,1)}) custom-call(bf16[2,512,1024]{2,1,0:T(8,128)(2,1)} %bitcast.8, bf16[2,512,1024]{2,1,0:T(8,128)(2,1)} %bitcast.11, bf16[64,1024]{1,0:T(8,128)(2,1)} %wsh.1, ...), custom_call_target="tpu_custom_call" | custom-call | tf_op jit(solution)/shard_map/pallas_call | solution.py:383
  217.1 8.3 %shard_map.93 = (bf16[2,512,1024]{2,1,0:T(8,128)(2,1)}, bf16[2,512,1024]{2,1,0:T(8,128)(2,1)}, bf16[2,512,512]{2,1,0:T(8,128)(2,1)}, f32[64,1024]{1,0:T(8,128)}, bf16[1024,32]{1,0:T(8,128)(2,1)}) custom-call(bf16[2,512,1024]{2,1,0:T(8,128)(2,1)} %bitcast.9, bf16[2,512,512]{2,1,0:T(8,128)(2,1)} %left.1, bf16[2,512,1024]{2,1,0:T(8,128)(2,1)} %bitcast.10, ...), custom_call_target="tpu_custom_call" | custom-call | tf_op jit(solution)/shard_map/pallas_call | solution.py:433

commit v3 on v2

--- a/solution.py
+++ b/solution.py
@@ -170,17 +170,19 @@
         return carry
 
     lax.fori_loop(0, blocks * row_tiles, first_tile, 0)
+    def send_first(k):
+        each(functools.partial(to_cols, 0, k, first_s, fc), "start")
+        fc[k, pl.ds(me * blocks, blocks)] = first_s[:, me * chunks + k]
+
+    def send_second_grad(k):
+        each(functools.partial(to_cols, 1, k, sg_s, gc), "start")
+        gc[k, pl.ds(me * blocks, blocks)] = sg_s[:, me * chunks + k]
+
+    send_first(0)
     w_far.wait_recv()
     w_pass.start()
-    for k in range(chunks):
-        if k == 1:
-            loads[2].wait()
-            w_near.wait_recv()
-            w_pass.wait_recv()
-            for d in range(1, PLANE):
-                w_q(d).start()
-        each(functools.partial(to_cols, 0, k, first_s, fc), "start")
-        fc[k, pl.ds(me * blocks, blocks)] = first_s[:, me * chunks + k]
+    for k in range(1, chunks):
+        send_first(k)
 
     spread = (
         lax.broadcasted_iota(jnp.int32, (deep // ROWS, deep), 1) // ROWS
@@ -199,6 +201,39 @@
         wide = jnp.dot(rk, spread, preferred_element_type=F32)
         mix[k] = jnp.where(same, wide, 0.0).astype(BF16)
 
+    def mixed(k, src, dst, dims):
+        def step(t, carry):
+            cols = pl.ds(pl.multiple_of(t * tile, tile), tile)
+            x = src[k, :, :, cols].reshape(deep, tile)
+            y = lax.dot_general(mix[k], x, (dims, ((), ())), preferred_element_type=F32)
+            dst[k, :, :, cols] = y.astype(BF16).reshape(deep // ROWS, ROWS, tile)
+            return carry
+
+        lax.fori_loop(0, width // tile, step, 0)
+
+    def second_of(k):
+        each(functools.partial(to_cols, 0, k, first_s, fc), "recv")
+        mixed(k, fc, sc, ((1,), (0,)))
+        each(functools.partial(to_rows_, 2, k, sc, sr), "start")
+        sr[:, me * chunks + k] = sc[k, pl.ds(me * blocks, blocks)]
+
+    def first_grad_of(k):
+        each(functools.partial(to_cols, 1, k, sg_s, gc), "recv")
+        mixed(k, gc, fgc, ((0,), (0,)))
+        each(functools.partial(to_rows_, 3, k, fgc, fr), "start")
+        pltpu.make_async_copy(
+            fgc.at[k, pl.ds(me * blocks, blocks)], fr.at[:, me * chunks + k], lsem.at[4 + k]
+        ).start()
+
+    second_of(0)
+    loads[2].wait()
+    w_near.wait_recv()
+    w_pass.wait_recv()
+    for d in range(1, PLANE):
+        w_q(d).start()
+    for k in range(1, chunks):
+        second_of(k)
+
     for d in range(1, PLANE):
         w_q(d).wait_recv()
     loads[3].wait()
@@ -215,32 +250,88 @@
         return carry
 
     lax.fori_loop(0, blocks * row_tiles, gate_tile, 0)
+    send_second_grad(0)
+
     for k in range(chunks):
-        each(functools.partial(to_cols, 1, k, sg_s, gc), "start")
-        gc[k, pl.ds(me * blocks, blocks)] = sg_s[:, me * chunks + k]
-
-    def mixed(k, src, dst, dims):
-        def step(t, carry):
-            cols = pl.ds(pl.multiple_of(t * tile, tile), tile)
-            x = src[k, :, :, cols].reshape(deep, tile)
-            y = lax.dot_general(mix[k], x, (dims, ((), ())), preferred_element_type=F32)
-            dst[k, :, :, cols] = y.astype(BF16).reshape(deep // ROWS, ROWS, tile)
-            return carry
-
-        lax.fori_loop(0, width // tile, step, 0)
-
-    for k in range(chunks):
-        each(functools.partial(to_cols, 0, k, first_s, fc), "recv")
-        mixed(k, fc, sc, ((1,), (0,)))
-        each(functools.partial(to_rows_, 2, k, sc, sr), "start")
-        sr[:, me * chunks + k] = sc[k, pl.ds(me * blocks, blocks)]
-    for k in range(chunks):
-        each(functools.partial(to_cols, 1, k, sg_s, gc), "recv")
-        mixed(k, gc, fgc, ((0,), (0,)))
-        each(functools.partial(to_rows_, 3, k, fgc, fr), "start")
-        pltpu.make_async_copy(
-            fgc.at[k, pl.ds(me * blocks, blocks)], fr.at[:, me * chunks + k], lsem.at[4 + k]
-        ).start()
+        each(functools.partial(to_rows_, 2, k, sc, sr), "recv")
+
+    def delta_tile(t, carry):
+        a, j = t // row_tiles, t % row_tiles
+        rows = pl.ds(j * tile, tile)
+        gf = gate[a, rows, :].astype(F32)
+        sig = jax.nn.sigmoid(gf)
+        sec = sr[a, pl.ds(j * per, per)].reshape(tile, width).astype(F32)
+        up = cot[a, rows, :].astype(F32)
+        out[a, rows, :] = (sec * (gf * sig)).astype(BF16)
+        delta[a, rows, :] = (up * sec * (sig * (1.0 + gf * (1.0 - sig)))).astype(BF16)
+        return carry
+
+    lax.fori_loop(0, blocks * row_tiles, delta_tile, 0)
+    out_copy = pltpu.make_async_copy(out, out_hbm, lsem.at[0])
+    out_copy.start()
+
+    def weight_tile(z, carry):
+        cols = pl.ds(pl.multiple_of(z * tile, tile), tile)
+        tokens_2d = tok[:, :, cols].reshape(blocks * tok.shape[1], tile)
+        delta_2d = delta[...].reshape(blocks * tok.shape[1], width)
+        prod = lax.dot_general(tokens_2d, delta_2d, (((0,), (0,)), ((), ())), preferred_element_type=F32)
+        wt[z] = prod.astype(BF16).reshape(PLANE, tile // PLANE, width)
+        return carry
+
+    lax.fori_loop(0, width // tile, weight_tile, 0)
+
+    def g_q(d):
+        peer = (qi + d) % PLANE
+        return remote(wt.at[:, peer], half.at[d - 1], gs_sem.at[0, d], gr_sem.at[0, d], zi * PLANE + peer)
+
+    g_near = [
+        remote(quarter.at[beside], tail.at[0], gs_sem.at[1, 0], gr_sem.at[1, 0], beside * PLANE + qi),
+        remote(
+            quarter.at[(beside + nz // 2) % nz], tail.at[1], gs_sem.at[1, 1], gr_sem.at[1, 1], beside * PLANE + qi
+        ),
+    ]
+    g_far = remote(pair, tail.at[2], gs_sem.at[1, 2], gr_sem.at[1, 2], across * PLANE + qi)
+
+    for d in range(1, PLANE):
+        g_q(d).start()
+
+    for k in range(1, chunks):
+        send_second_grad(k)
+
+    for d in range(1, PLANE):
+        g_q(d).wait_recv()
+
+    def sum_tile(z, carry):
+        total = wt[z, qi].astype(F32)
+        for d in range(PLANE - 1):
+            total = total + half[d, z].astype(F32)
+        quarter[z] = total.astype(BF16)
+        return carry
+
+    lax.fori_loop(0, nz, sum_tile, 0)
+    for copy in g_near:
+        copy.start()
+    first_grad_of(0)
+
+    for copy in g_near:
+        copy.wait_recv()
+    pair[...] = (quarter[across].astype(F32) + tail[1].astype(F32)).astype(BF16)
+    g_far.start()
+    for k in range(1, chunks):
+        first_grad_of(k)
+
+    def part_tile(t, carry):
+        a, j = t // row_tiles, t % row_tiles
+        rows = pl.ds(j * tile, tile)
+        weight = wf[...].reshape(width, width)
+        part[a, rows, :] = lax.dot_general(
+            delta[a, rows, :], weight, (((1,), (1,)), ((), ())), preferred_element_type=F32
+        ).astype(BF16)
+        return carry
+
+    lax.fori_loop(0, blocks * row_tiles, part_tile, 0)
+    part_copy = pltpu.make_async_copy(part, part_hbm, lsem.at[1])
+    part_copy.start()
 
     scale_w = width ** (-0.5)
     for k in range(chunks):
@@ -256,79 +347,6 @@
             turn, picked, (((0,), (0,)), ((), ())), preferred_element_type=F32
         ).astype(BF16)
 
-    for k in range(chunks):
-        each(functools.partial(to_rows_, 2, k, sc, sr), "recv")
-
-    def delta_tile(t, carry):
-        a, j = t // row_tiles, t % row_tiles
-        rows = pl.ds(j * tile, tile)
-        gf = gate[a, rows, :].astype(F32)
-        sig = jax.nn.sigmoid(gf)
-        sec = sr[a, pl.ds(j * per, per)].reshape(tile, width).astype(F32)
-        up = cot[a, rows, :].astype(F32)
-        out[a, rows, :] = (sec * (gf * sig)).astype(BF16)
-        delta[a, rows, :] = (up * sec * (sig * (1.0 + gf * (1.0 - sig)))).astype(BF16)
-        return carry
-
-    lax.fori_loop(0, blocks * row_tiles, delta_tile, 0)
-    out_copy = pltpu.make_async_copy(out, out_hbm, lsem.at[0])
-    out_copy.start()
-
-    def weight_tile(z, carry):
-        cols = pl.ds(pl.multiple_of(z * tile, tile), tile)
-        tokens_2d = tok[:, :, cols].reshape(blocks * tok.shape[1], tile)
-        delta_2d = delta[...].reshape(blocks * tok.shape[1], width)
-        prod = lax.dot_general(tokens_2d, delta_2d, (((0,), (0,)), ((), ())), preferred_element_type=F32)
-        wt[z] = prod.astype(BF16).reshape(PLANE, tile // PLANE, width)
-        return carry
-
-    lax.fori_loop(0, width // tile, weight_tile, 0)
-
-    def g_q(d):
-        peer = (qi + d) % PLANE
-        return remote(wt.at[:, peer], half.at[d - 1], gs_sem.at[0, d], gr_sem.at[0, d], zi * PLANE + peer)
-
-    g_near = [
-        remote(quarter.at[beside], tail.at[0], gs_sem.at[1, 0], gr_sem.at[1, 0], beside * PLANE + qi),
-        remote(
-            quarter.at[(beside + nz // 2) % nz], tail.at[1], gs_sem.at[1, 1], gr_sem.at[1, 1], beside * PLANE + qi
-        ),
-    ]
-    g_far = remote(pair, tail.at[2], gs_sem.at[1, 2], gr_sem.at[1, 2], across * PLANE + qi)
-
-    for d in range(1, PLANE):
-        g_q(d).start()
-
-    def part_tile(t, carry):
-        a, j = t // row_tiles, t % row_tiles
-        rows = pl.ds(j * tile, tile)
-        weight = wf[...].reshape(width, width)
-        part[a, rows, :] = lax.dot_general(
-            delta[a, rows, :], weight, (((1,), (1,)), ((), ())), preferred_element_type=F32
-        ).astype(BF16)
-        return carry
-
-    lax.fori_loop(0, blocks * row_tiles, part_tile, 0)
-    part_copy = pltpu.make_async_copy(part, part_hbm, lsem.at[1])
-    part_copy.start()
-
-    for d in range(1, PLANE):
-        g_q(d).wait_recv()
-
-    def sum_tile(z, carry):
-        total = wt[z, qi].astype(F32)
-        for d in range(PLANE - 1):
-            total = total + half[d, z].astype(F32)
-        quarter[z] = total.astype(BF16)
-        return carry
-
-    lax.fori_loop(0, nz, sum_tile, 0)
-    for copy in g_near:
-        copy.start()
-    for copy in g_near:
-        copy.wait_recv()
-    pair[...] = (quarter[across].astype(F32) + tail[1].astype(F32)).astype(BF16)
-    g_far.start()
     g_far.wait_recv()
     total = quarter[zi].astype(F32) + tail[0].astype(F32) + tail[2].astype(F32)
     ggrad[...] = total * (blocks * tok.shape[1] * n) ** (-0.5)

time: 228 us -> 212 us (0.930)
  Pallas kernels: 225 us -> 208 us
    pallas_call x1, Pallas kernels: 216 us -> 199 us  [fused_body(): pl.pallas_call(functools.partial(mixer_kernel, n), out_shape=(jax.ShapeDt...]
where the time goes in v3:
time: 212 us; the launch traced here: 208 us
  Pallas kernels  208 us (98%)
    pallas_call x1, Pallas kernels, fused_body(): pl.pallas_call(functools.partial(mixer_kernel, n), out_shape=(jax.ShapeDt...  199 us
    pallas_call x1, Pallas kernels, fused_body(): pl.pallas_call(functools.partial(last_kernel, width ** (-0.5)), grid=(ste...  8.31 us

profile of v3, /device:TPU:13, one launch (start us, length us, event | category | flops | bytes accessed | tf_op | source)
XLA Modules:
  0.0 208.3 jit_solution(16231895081472534217)
XLA Ops:
  0.6 199.4 %shard_map.92 = (bf16[2,512,1024]{2,1,0:T(8,128)(2,1)}, bf16[2,512,1024]{2,1,0:T(8,128)(2,1)}, bf16[2,32,16,1024]{3,2,1,0:T(8,128)(2,1)}, f32[64,1024]{1,0:T(8,128)}, bf16[2,512,32]{2,1,0:T(8,128)(2,1)}) custom-call(bf16[2,512,1024]{2,1,0:T(8,128)(2,1)} %bitcast.8, bf16[2,512,1024]{2,1,0:T(8,128)(2,1)} %bitcast.11, bf16[64,1024]{1,0:T(8,128)(2,1)} %wsh.1, ...), custom_call_target="tpu_custom_call" | custom-call | tf_op jit(solution)/shard_map/pallas_call | solution.py:401
  200.0 8.3 %shard_map.93 = (bf16[2,512,1024]{2,1,0:T(8,128)(2,1)}, bf16[2,512,1024]{2,1,0:T(8,128)(2,1)}, bf16[2,512,512]{2,1,0:T(8,128)(2,1)}, f32[64,1024]{1,0:T(8,128)}, bf16[1024,32]{1,0:T(8,128)(2,1)}) custom-call(bf16[2,512,1024]{2,1,0:T(8,128)(2,1)} %bitcast.9, bf16[2,512,512]{2,1,0:T(8,128)(2,1)} %left.1, bf16[2,512,1024]{2,1,0:T(8,128)(2,1)} %bitcast.10, ...), custom_call_target="tpu_custom_call" | custom-call | tf_op jit(solution)/shard_map/pallas_call | solution.py:451

commit v4 on v3

--- a/solution.py
+++ b/solution.py
@@ -123,7 +123,7 @@
         t = (s * 7) % n
         peer = (me + t) % n
         return remote(
-            src.at[:, peer * chunks + k], dst.at[k, pl.ds(me * blocks, blocks)],
+            src.at[:, peer, k], dst.at[k, pl.ds(me * blocks, blocks)],
             ssem.at[ph, k, t], rsem.at[ph, k, t], peer,
         )
 
@@ -163,20 +163,23 @@
     loads[0].wait()
     loads[1].wait()
 
-    def first_tile(t, carry):
-        a, j = t // row_tiles, t % row_tiles
-        prod = jnp.dot(left[a, pl.ds(j * tile, tile), :], tok[a], preferred_element_type=F32)
-        first_s[a, pl.ds(j * per, per)] = prod.astype(BF16).reshape(per, ROWS, width)
-        return carry
-
-    lax.fori_loop(0, blocks * row_tiles, first_tile, 0)
+    def first_tile(k):
+        def step(a, carry):
+            lhs = left[a, :, k].reshape(n * ROWS, left.shape[4])
+            prod = jnp.dot(lhs, tok[a], preferred_element_type=F32)
+            first_s[a, :, k] = prod.astype(BF16).reshape(n, ROWS, width)
+            return carry
+
+        lax.fori_loop(0, blocks, step, 0)
+
     def send_first(k):
+        first_tile(k)
         each(functools.partial(to_cols, 0, k, first_s, fc), "start")
-        fc[k, pl.ds(me * blocks, blocks)] = first_s[:, me * chunks + k]
+        fc[k, pl.ds(me * blocks, blocks)] = first_s[:, me, k]
 
     def send_second_grad(k):
         each(functools.partial(to_cols, 1, k, sg_s, gc), "start")
-        gc[k, pl.ds(me * blocks, blocks)] = sg_s[:, me * chunks + k]
+        gc[k, pl.ds(me * blocks, blocks)] = sg_s[:, me, k]
 
     send_first(0)
     w_far.wait_recv()
@@ -246,7 +249,8 @@
         gate[a, rows, :] = g
         gf = g.astype(F32)
         up = cot[a, rows, :].astype(F32) * (gf * jax.nn.sigmoid(gf))
-        sg_s[a, pl.ds(j * per, per)] = up.astype(BF16).reshape(per, ROWS, width)
+        sends = per // chunks
+        sg_s[a, pl.ds(j * sends, sends)] = up.astype(BF16).reshape(sends, chunks, ROWS, width)
         return carry
 
     lax.fori_loop(0, blocks * row_tiles, gate_tile, 0)
@@ -394,6 +398,7 @@
     shard = width // n
     rows = (blocks, inner, width)
     by_row = pltpu.VMEM((blocks, groups, ROWS, width), BF16)
+    by_peer = pltpu.VMEM((blocks, n, chunks, ROWS, width), BF16)
     by_col = pltpu.VMEM((chunks, outer, ROWS, width), BF16)
     vmem = pl.BlockSpec(memory_space=pltpu.VMEM)
     hbm = pl.BlockSpec(memory_space=pltpu.HBM)
@@ -412,11 +417,11 @@
         scratch_shapes=[
             pltpu.VMEM(rows, BF16),
             pltpu.VMEM(rows, BF16),
-            pltpu.VMEM((blocks, inner, inner), BF16),
+            pltpu.VMEM((blocks, n, chunks, ROWS, inner), BF16),
             pltpu.VMEM(rows, BF16),
             pltpu.VMEM(rows, BF16),
             pltpu.VMEM((nz, PLANE, shard, width), BF16),
-            by_row, by_row, by_col, by_col, by_col, by_col, by_row,
+            by_peer, by_peer, by_col, by_col, by_col, by_col, by_row,
             pltpu.VMEM(rows, BF16),
             pltpu.VMEM(rows, BF16),
             pltpu.VMEM((nz, PLANE, shard, width), BF16),
@@ -437,7 +442,8 @@
             collective_id=0, has_side_effects=True, vmem_limit_bytes=60 * 2**20
         ),
     )(
-        token_grid, cotangent.reshape(rows), gate_weight, left_blocks, right_blocks.reshape(chunks, deep, outer)
+        token_grid, cotangent.reshape(rows), gate_weight,
+        left_blocks.reshape(blocks, n, chunks, ROWS, inner), right_blocks.reshape(chunks, deep, outer),
     )
     size = 256
     per_block = inner // size

time: 212 us -> 212 us (level)
  no operation moved by 1% of the time
where the time goes in v4:
time: 212 us; the launch traced here: 208 us
  Pallas kernels  208 us (98%)
    pallas_call x1, Pallas kernels, fused_body(): pl.pallas_call(functools.partial(mixer_kernel, n), out_shape=(jax.ShapeDt...  199 us
    pallas_call x1, Pallas kernels, fused_body(): pl.pallas_call(functools.partial(last_kernel, width ** (-0.5)), grid=(ste...  8.31 us

profile of v4, /device:TPU:13, one launch (start us, length us, event | category | flops | bytes accessed | tf_op | source)
XLA Modules:
  0.0 208.3 jit_solution(15815312151810688910)
XLA Ops:
  0.6 199.4 %shard_map.92 = (bf16[2,512,1024]{2,1,0:T(8,128)(2,1)}, bf16[2,512,1024]{2,1,0:T(8,128)(2,1)}, bf16[2,32,16,1024]{3,2,1,0:T(8,128)(2,1)}, f32[64,1024]{1,0:T(8,128)}, bf16[2,512,32]{2,1,0:T(8,128)(2,1)}) custom-call(bf16[2,512,1024]{2,1,0:T(8,128)(2,1)} %bitcast.9, bf16[2,512,1024]{2,1,0:T(8,128)(2,1)} %bitcast.13, bf16[64,1024]{1,0:T(8,128)(2,1)} %wsh.1, ...), custom_call_target="tpu_custom_call" | custom-call | tf_op jit(solution)/shard_map/pallas_call | solution.py:406
  200.0 8.3 %shard_map.93 = (bf16[2,512,1024]{2,1,0:T(8,128)(2,1)}, bf16[2,512,1024]{2,1,0:T(8,128)(2,1)}, bf16[2,512,512]{2,1,0:T(8,128)(2,1)}, f32[64,1024]{1,0:T(8,128)}, bf16[1024,32]{1,0:T(8,128)(2,1)}) custom-call(bf16[2,512,1024]{2,1,0:T(8,128)(2,1)} %bitcast.10, bf16[2,512,512]{2,1,0:T(8,128)(2,1)} %left.1, bf16[2,512,1024]{2,1,0:T(8,128)(2,1)} %bitcast.12, ...), custom_call_target="tpu_custom_call" | custom-call | tf_op jit(solution)/shard_map/pallas_call | solution.py:457
